TPU v7x, 256 devices: a whole 4x4x8 slice. The times are simulated.
256 devices in a mesh: grp: 8 (over z_hi, y), sp: 32 (over z_lo, x, core).
Axes of the slice: x: 4, y: 4, z: 8 (z_hi: 2, z_lo: 4; z = z_hi * 4 + z_lo), core: 2. Of those that a mesh axis runs over, the one named last changes fastest.
Arguments:
- alpha: float32 [80, 32, 4096], P('grp', None, 'sp'), may hold values from -6 to 6
- ensemble: bfloat16 [80, 3, 32, 4096], P('grp', None, None, 'sp'), may hold values from -6 to 6
- static_std: float32 [3, 32, 4096], P(None, 'grp', 'sp'), may hold values from 0.2 to 1
- control: float32 [3, 32, 4096], P(None, 'grp', 'sp'), may hold values from -6 to 6
- loc_spectrum: float32 [1024], replicated, may hold values from 0.00024414062 to 0.001953125
- obs_cell: int32 [262144], P(('grp', 'sp')), may hold values from 0 to 131071, as said below
- obs_step: int32 [262144], P(('grp', 'sp')), may hold values from 0 to 2
- innovation: float32 [262144], P(('grp', 'sp')), may hold values from -6 to 6
- obs_weight: float32 [262144], P(('grp', 'sp')), may hold values from 0.5 to 4
Outputs:
- grad_alpha: float32 [80, 32, 4096], P('grp', None, 'sp')
- grad_control: float32 [3, 32, 4096], P(None, 'grp', 'sp')
Inputs may be any that keep to these rules, and one draw needn't show every extreme that they name: `obs_cell`: an entry is row * 4096 + column. Entries 1024 * b to 1024 * (b + 1) - 1 lie in the tile of 4 rows from row 4 * (b // 32) and 128 columns from column 128 * (b % 32).
All inputs are finite; a program needn't handle non-finite values.
Results may differ from a plain program's by a relative error of at most 0.0075.
Values may be sent and summed in bfloat16 or wider, within the bound.
No kernel may reach another device: no remote copies, remote signals or barrier semaphores. Data moves between devices by JAX's collectives and lax.ppermute only.
A program may use at most 128 MiB of HBM per device.

v0:
```python
import math
import jax
import jax.numpy as jnp
from jax import lax
from jax.sharding import Mesh
from jax.sharding import PartitionSpec as P

NX = 4096
GRP_SP = ("grp", "sp_0", "sp_1", "sp_2")
SP = ("sp_0", "sp_1", "sp_2")
courant = 0.4


def extended(block, sides, width):
    for axis, dim in sides:
        count = lax.axis_size(axis)
        forward = [(i, i + 1) for i in range(count - 1)]
        forward.append((count - 1, 0))
        backward = [(target, source) for source, target in forward]
        low = lax.ppermute(
            lax.slice_in_dim(block, block.shape[dim] - width, None, axis=dim), axis, forward
        )
        high = lax.ppermute(lax.slice_in_dim(block, 0, width, axis=dim), axis, backward)
        block = jnp.concatenate([low, block, high], axis=dim)
    return block


def in_blocks(x, dim, length):
    shape = x.shape
    tiles = x.reshape(*shape[:dim], length, shape[dim] // length, *shape[dim + 1 :])
    return jnp.moveaxis(tiles, dim, 0)


def sum_at_owner(x, axis, dim):
    tiles = in_blocks(x, dim, lax.axis_size(axis))
    arrived = lax.all_to_all(tiles, axis, split_axis=0, concat_axis=0, tiled=True)
    return arrived.sum(axis=0)


def in_order(tiles, dim):
    tiles = jnp.moveaxis(tiles, 0, dim)
    shape = tiles.shape
    return tiles.reshape(*shape[:dim], shape[dim] * shape[dim + 1], *shape[dim + 2 :])


def copy_for_each(x, axis):
    copies = jnp.broadcast_to(x, (lax.axis_size(axis), *x.shape))
    return lax.all_to_all(copies, axis, split_axis=0, concat_axis=0, tiled=True)


def gathered_copies(x, axis, dim):
    return in_order(copy_for_each(x, axis), dim)


def moved_by_axis(tiles, axes, turns):
    shape = [lax.axis_size(a) for a in axes]
    tiles = tiles.reshape(*shape, *tiles.shape[1:])
    for k in turns:
        tiles = lax.all_to_all(tiles, axes[k], split_axis=k, concat_axis=k, tiled=True)
    return tiles.reshape(-1, *tiles.shape[len(axes) :])


def core_and_chips(x, groups, turns, split_dim, concat_dim):
    length = lax.axis_size(groups[0]) * lax.axis_size(groups[1])
    tiles = in_blocks(x, split_dim, length)
    return in_order(moved_by_axis(tiles, groups, turns), concat_dim)


def spectral_filter(rows_data, loc_spectrum):
    length_x = rows_data.shape[1]
    kept_waves = loc_spectrum.shape[0]
    freq_block = math.gcd(kept_waves, 256)
    positions = jnp.arange(length_x, dtype=jnp.int32)
    filtered = jnp.zeros(rows_data.shape, jnp.float32)
    for start_wave in range(0, kept_waves, freq_block):
        waves = start_wave + jnp.arange(freq_block, dtype=jnp.int32)
        phases = positions[:, None] * waves[None, :] % length_x
        radians = 2.0 * math.pi / length_x * phases.astype(jnp.float32)
        fourier_basis = jnp.concatenate([jnp.cos(radians), jnp.sin(radians)], axis=1)
        weights = loc_spectrum[start_wave : start_wave + freq_block]
        weights = jnp.concatenate([weights, weights])
        coeffs = jnp.dot(
            rows_data,
            fourier_basis,
            precision=lax.Precision.HIGHEST,
            preferred_element_type=jnp.float32,
        )
        filtered = filtered + jnp.dot(
            coeffs * weights[None, :],
            fourier_basis.T,
            precision=lax.Precision.HIGHEST,
            preferred_element_type=jnp.float32,
        )
    return filtered


def inner(field):
    return field[..., 1:-1, 1:-1]


def diff_x(field):
    return 0.5 * (field[..., 1:-1, 2:] - field[..., 1:-1, :-2])


def diff_y(field):
    return 0.5 * (field[..., 2:, 1:-1] - field[..., :-2, 1:-1])


def clip_rows(stack, margin, first_row, total_rows):
    rows_index = first_row - margin + jnp.arange(stack.shape[1], dtype=jnp.int32)
    valid = jnp.logical_and(rows_index >= 0, rows_index < total_rows).astype(jnp.float32)
    return stack * valid[None, :, None]


def coriolis_rows(first_row, margin, count, total_rows):
    rows_index = first_row - margin + jnp.arange(count, dtype=jnp.int32)
    return (0.1 + 0.2 * (rows_index.astype(jnp.float32) + 0.5) / total_rows)[:, None]


def forward_a(stack, margin, first_row, total_rows):
    height, eastward, northward = (stack[0], stack[1], stack[2])
    new_height = inner(height) - courant * (diff_x(eastward) + diff_y(northward))
    result = jnp.stack([new_height, inner(eastward), inner(northward)])
    return clip_rows(result, margin - 1, first_row, total_rows)


def forward_b(stack, margin, first_row, total_rows):
    height, eastward, northward = (stack[0], stack[1], stack[2])
    rotation = coriolis_rows(first_row, margin - 1, stack.shape[1] - 2, total_rows)
    new_east = inner(eastward) - courant * diff_x(height) + rotation * inner(northward)
    new_north = inner(northward) - courant * diff_y(height) - rotation * inner(eastward)
    result = jnp.stack([inner(height), new_east, new_north])
    return clip_rows(result, margin - 1, first_row, total_rows)


def backward_a(stack, margin, first_row, total_rows):
    back_h, back_u, back_w = (stack[0], stack[1], stack[2])
    adj_height = inner(back_h) + courant * (diff_x(back_u) + diff_y(back_w))
    result = jnp.stack([adj_height, inner(back_u), inner(back_w)])
    return clip_rows(result, margin - 1, first_row, total_rows)


def backward_b(stack, margin, first_row, total_rows):
    adj_height, back_u, back_w = (stack[0], stack[1], stack[2])
    rotation = coriolis_rows(first_row, margin - 1, stack.shape[1] - 2, total_rows)
    adj_east = inner(back_u) - rotation * inner(back_w) + courant * diff_x(adj_height)
    adj_north = inner(back_w) + rotation * inner(back_u) + courant * diff_y(adj_height)
    result = jnp.stack([inner(adj_height), adj_east, adj_north])
    return clip_rows(result, margin - 1, first_row, total_rows)


def deep_rim(stack):
    return extended(stack, (("grp", 1), (SP, 2)), 4)


def per_device(
    alpha, ensemble, static_std, control, loc_spectrum, obs_cell, obs_step, innovation, obs_weight
):
    members_local = alpha.shape[0]
    groups = lax.axis_size("grp")
    spread = 1.0 / math.sqrt(members_local * groups - 1)
    tile_rows, tile_cols = (control.shape[1], control.shape[2])
    total_rows = tile_rows * groups
    first_row = lax.axis_index("grp") * tile_rows
    first_col = lax.axis_index(SP) * tile_cols

    def localize_items(items):
        dims = items.shape
        flat = items.reshape(dims[0] * dims[1], dims[2])
        return spectral_filter(flat, loc_spectrum).reshape(dims)

    def to_rows(columns):
        return localize_items(lax.all_to_all(columns, SP, split_axis=1, concat_axis=2, tiled=True))

    localized = lax.all_to_all(
        to_rows(alpha).astype(jnp.bfloat16), SP, split_axis=2, concat_axis=1, tiled=True
    )
    partial_value = jnp.einsum(
        "mvyx,myx->vyx", ensemble, localized, preferred_element_type=jnp.float32
    )
    summed = sum_at_owner(partial_value, "grp", 1)
    increment = static_std * control + spread * summed
    padded = clip_rows(deep_rim(increment), 4, first_row, total_rows)
    middle = forward_b(forward_a(padded, 4, first_row, total_rows), 3, first_row, total_rows)
    first_state = middle[:, 2:-2, 2:-2]
    second_state = forward_b(forward_a(middle, 2, first_row, total_rows), 1, first_row, total_rows)
    states = (increment, first_state, second_state)
    local_index = (obs_cell // NX - first_row) * tile_cols + (obs_cell % NX - first_col)
    observed = jnp.zeros(innovation.shape, jnp.float32)
    for moment in range(3):
        values = states[moment][0].reshape(-1)[local_index]
        observed = jnp.where(obs_step == moment, values, observed)
    misfit = obs_weight * (observed - innovation)
    forcings = []
    for moment in range(3):
        spread_obs = jnp.where(obs_step == moment, misfit, jnp.zeros_like(misfit))
        height_force = (
            jnp.zeros((tile_rows * tile_cols,), jnp.float32).at[local_index].add(spread_obs)
        )
        forcings.append(height_force.reshape(tile_rows, tile_cols))
    zero_field = jnp.zeros((tile_rows, tile_cols), jnp.float32)
    last_adjoint = jnp.stack([forcings[2], zero_field, zero_field])
    padded = clip_rows(
        deep_rim(jnp.concatenate([last_adjoint, forcings[1][None]], axis=0)),
        4,
        first_row,
        total_rows,
    )
    middle = backward_b(backward_a(padded[:3], 4, first_row, total_rows), 3, first_row, total_rows)
    middle = middle.at[0].add(padded[3, 2:-2, 2:-2])
    adjoint = backward_b(backward_a(middle, 2, first_row, total_rows), 1, first_row, total_rows)
    adjoint = adjoint.at[0].add(forcings[0])
    grad_control = control + static_std * adjoint
    half = adjoint.astype(jnp.bfloat16)
    weighted = jnp.einsum(
        "mvyx,vyx->myx",
        ensemble,
        gathered_copies(half, "grp", 1),
        preferred_element_type=jnp.float32,
    )
    filtered = core_and_chips(to_rows(weighted), (("sp_0", "sp_1"), "sp_2"), (1, 0), 2, 1)
    grad_alpha = alpha + spread * filtered
    return (grad_alpha, grad_control)


def solution(mesh):
    torus = Mesh(mesh.devices.reshape(mesh.shape["grp"], 4, 4, 2), ("grp", "sp_0", "sp_1", "sp_2"))
    placed = (
        P("grp", None, SP),
        P("grp", None, None, SP),
        P(None, "grp", SP),
        P(None, "grp", SP),
        P(),
        P(GRP_SP),
        P(GRP_SP),
        P(GRP_SP),
        P(GRP_SP),
    )
    return jax.shard_map(
        per_device,
        mesh=torus,
        in_specs=placed,
        out_specs=(P("grp", None, SP), P(None, "grp", SP)),
        check_vma=False,
    )
```

profile of v0, /device:TPU:1, one launch (start us, length us, event | category | flops | bytes accessed | tf_op | source)
XLA Modules:
  0.0 377.0 jit_solution(4057525190884514991)
XLA Ops:
  0.6 1.7 copy.25
  2.4 10.0 %all-to-all-start = ((f32[10,32,128]{2,0,1:T(8,128)}), f32[10,32,128]{2,0,1:T(8,128)S(1)}, u32[]{:S(2)}, u32[]{:S(2)}) async-start(f32[10,32,128]{2,0,1:T(8,128)} %copy.25), calls=%async_computation | async-start | bytes 524288 | tf_op jit(solution)/shard_map/all_to_all | solution.py:173
  12.4 17.6 %fusion.36 = (f32[4096,256]{1,0:T(8,128)}, f32[4096,256]{1,0:T(8,128)}) fusion(), kind=kLoop, calls=%fused_computation.64 | loop fusion | flops 14680064 | bytes 8388608 | tf_op jit(solution)/shard_map/sin | solution.py:79
  30.1 17.9 %fusion.43 = (f32[4096,256]{1,0:T(8,128)}, f32[4096,256]{1,0:T(8,128)}) fusion(s32[256]{0:T(256)S(1)} %iota_add_fusion.2), kind=kLoop, calls=%fused_computation.71 | loop fusion | flops 14680064 | bytes 8389632 | tf_op jit(solution)/shard_map/cos | solution.py:79
  47.9 17.9 %fusion.41 = (f32[4096,256]{1,0:T(8,128)}, f32[4096,256]{1,0:T(8,128)}) fusion(s32[256]{0:T(256)S(1)} %iota_add_fusion.1), kind=kLoop, calls=%fused_computation.69 | loop fusion | flops 14680064 | bytes 8389632 | tf_op jit(solution)/shard_map/cos | solution.py:79
  65.8 17.9 %fusion.39 = (f32[4096,256]{1,0:T(8,128)}, f32[4096,256]{1,0:T(8,128)}) fusion(s32[256]{0:T(256)S(1)} %iota_add_fusion), kind=kLoop, calls=%fused_computation.67 | loop fusion | flops 14680064 | bytes 8389632 | tf_op jit(solution)/shard_map/cos | solution.py:79
  84.1 7.5 %fusion.44 = f32[512,10]{0,1:T(8,128)S(1)} fusion(f32[10,4096]{1,0:T(8,128)S(1)} %bitcast.186, f32[4096,256]{1,0:T(8,128)} %get-tuple-element.102, f32[4096,256]{1,0:T(8,128)} %get-tuple-element.103, f32[512]{0:T(512)S(1)} %get-tuple-element.98), kind=kOutput, calls=%fused_computation.72 | convolution fusion | flops 253760512 | bytes 8574976 | tf_op jit(solution)/shard_map/dot_general | solution.py:82
  91.6 7.0 %fusion.34 = f32[10,4096]{1,0:T(8,128)S(1)} fusion(f32[512,10]{0,1:T(8,128)S(1)} %fusion.44, f32[4096,256]{1,0:T(8,128)S(1)} %copy-done, f32[4096,256]{1,0:T(8,128)S(1)} %copy-done.2), kind=kOutput, calls=%fused_computation.62 | convolution fusion | flops 253755392 | bytes 8572928 | tf_op jit(solution)/shard_map/dot_general | solution.py:88
  98.6 4.5 %fusion.46 = f32[512,10]{0,1:T(8,128)S(1)} fusion(f32[10,4096]{1,0:T(8,128)S(1)} %bitcast.187, f32[4096,256]{1,0:T(8,128)S(1)} %copy-done.14, f32[4096,256]{1,0:T(8,128)S(1)} %copy-done.12, f32[512]{0:T(512)S(1)} %get-tuple-element.99), kind=kOutput, calls=%fused_computation.74 | convolution fusion | flops 253760512 | bytes 8574976 | tf_op jit(solution)/shard_map/dot_general | solution.py:82
  103.1 7.2 %convolution_add_fusion.5 = f32[10,4096]{1,0:T(8,128)S(1)} fusion(f32[10,4096]{1,0:T(8,128)S(1)} %fusion.34, f32[512,10]{0,1:T(8,128)S(1)} %fusion.46, f32[4096,256]{1,0:T(8,128)S(1)} %copy-done.14, f32[4096,256]{1,0:T(8,128)S(1)} %copy-done.12), kind=kOutput, calls=%fused_computation.27 | convolution fusion | flops 253796352 | bytes 8736768 | tf_op jit(solution)/shard_map/dot_general | solution.py:88
  110.3 4.5 %fusion.48 = f32[512,10]{0,1:T(8,128)S(1)} fusion(f32[10,4096]{1,0:T(8,128)S(1)} %bitcast.188, f32[4096,256]{1,0:T(8,128)S(1)} %copy-done.10, f32[4096,256]{1,0:T(8,128)S(1)} %copy-done.8, f32[512]{0:T(512)S(1)} %get-tuple-element.100), kind=kOutput, calls=%fused_computation.76 | convolution fusion | flops 253760512 | bytes 8574976 | tf_op jit(solution)/shard_map/dot_general | solution.py:82
  114.9 7.2 %convolution_add_fusion.4 = f32[10,4096]{1,0:T(8,128)S(1)} fusion(f32[10,4096]{1,0:T(8,128)S(1)} %convolution_add_fusion.5, f32[512,10]{0,1:T(8,128)S(1)} %fusion.48, f32[4096,256]{1,0:T(8,128)S(1)} %copy-done.10, f32[4096,256]{1,0:T(8,128)S(1)} %copy-done.8), kind=kOutput, calls=%fused_computation.26 | convolution fusion | flops 253796352 | bytes 8736768 | tf_op jit(solution)/shard_map/dot_general | solution.py:88
  122.1 4.5 %fusion.50 = f32[512,10]{0,1:T(8,128)S(1)} fusion(f32[10,4096]{1,0:T(8,128)S(1)} %bitcast.189, f32[4096,256]{1,0:T(8,128)S(1)} %copy-done.6, f32[4096,256]{1,0:T(8,128)S(1)} %copy-done.4, f32[512]{0:T(512)S(1)} %get-tuple-element.101), kind=kOutput, calls=%fused_computation.78 | convolution fusion | flops 253760512 | bytes 8574976 | tf_op jit(solution)/shard_map/dot_general | solution.py:82
  126.6 7.4 %fusion.1 = bf16[10,1,4096]{2,0,1:T(8,128)(2,1)S(1)} fusion(f32[10,4096]{1,0:T(8,128)S(1)} %convolution_add_fusion.4, f32[512,10]{0,1:T(8,128)S(1)} %fusion.50, f32[4096,256]{1,0:T(8,128)S(1)} %copy-done.6, f32[4096,256]{1,0:T(8,128)S(1)} %copy-done.4), kind=kOutput, calls=%fused_computation.29 | convolution fusion | flops 253837312 | bytes 8654848 | tf_op jit(solution)/shard_map/dot_general | solution.py:88
  134.0 2.8 copy.27
  137.3 22.5 %reduce.8 = bf16[4096,10]{1,0:T(8,128)(2,1)S(1)} reduce(bf16[4096,1,10]{2,1,0:T(2,128)(2,1)S(1)} %bitcast.171, bf16[]{:T(256)} %broadcast.396), dimensions={1}, to_apply=%bitcast.152.reduce_sub_computation | reduce | bytes 163842
  159.8 2.5 reshape.241
  162.2 7.7 %all-to-all-start.1 = ((bf16[32,2,640]{2,1,0:T(2,128)(2,1)}), bf16[32,2,640]{2,1,0:T(2,128)(2,1)S(1)}, u32[]{:S(2)}, u32[]{:S(2)}) async-start(bf16[32,2,640]{2,1,0:T(2,128)(2,1)} %reshape.241), calls=%async_computation.1 | async-start | bytes 163840 | tf_op jit(solution)/shard_map/all_to_all | solution.py:175
  170.0 7.9 %all-to-all-done.1 = bf16[32,2,640]{2,1,0:T(2,128)(2,1)S(1)} async-done(((bf16[32,2,640]{2,1,0:T(2,128)(2,1)}), bf16[32,2,640]{2,1,0:T(2,128)(2,1)S(1)}, u32[]{:S(2)}, u32[]{:S(2)}) %all-to-all-start.1) | async-done | bytes 81952 | tf_op jit(solution)/shard_map/all_to_all | solution.py:175
  177.9 2.2 reshape.242
  180.1 2.1 copy.28
  183.0 8.1 %all-to-all-start.2 = ((f32[8,3,4,128]{3,2,1,0:T(4,128)}), f32[8,3,4,128]{3,2,1,0:T(4,128)S(1)}, u32[]{:S(2)}, u32[]{:S(2)}) async-start(f32[8,3,4,128]{3,2,1,0:T(4,128)} %copy.29), calls=%async_computation.2 | async-start | bytes 98304 | tf_op jit(solution)/shard_map/all_to_all | solution.py:36
  191.2 9.1 %all-to-all-done.2 = f32[8,3,4,128]{3,2,1,0:T(4,128)S(1)} async-done(((f32[8,3,4,128]{3,2,1,0:T(4,128)}), f32[8,3,4,128]{3,2,1,0:T(4,128)S(1)}, u32[]{:S(2)}, u32[]{:S(2)}) %all-to-all-start.2) | async-done | bytes 49184 | tf_op jit(solution)/shard_map/all_to_all | solution.py:36
  200.6 7.2 %collective-permute-start.1 = (f32[3,4,128]{2,1,0:T(4,128)S(1)}, f32[3,4,128]{2,1,0:T(4,128)S(1)}, u32[]{:S(2)}, u32[]{:S(2)}) collective-permute-start(f32[3,4,128]{2,1,0:T(4,128)S(1)} %multiply_add_fusion.1), channel_id=1, source_target_pairs={{32,0},{64,32},{96,64},{128,96},{160,128},{192,160},{224,192},{0,2... | collective-permute-start | bytes 18440 | tf_op jit(solution)/shard_map/ppermute | solution.py:23
  207.8 1.0 collective-permute-done
  208.9 3.1 collective-permute-start.2
  212.3 6.9 %gather_fusion.2 = f32[1024]{0:T(1024)S(1)} fusion(f32[512]{0:T(512)S(1)} %slice_bitcast_fusion.36, s32[1024]{0:T(1024)S(1)} %get-tuple-element.30), kind=kCustom, calls=%fused_computation.2 | custom fusion | bytes 12288 | tf_op jit(solution)/shard_map/gather | solution.py:191
  220.0 6.9 %gather_fusion = f32[1024]{0:T(1024)S(1)} fusion(f32[512]{0:T(512)S(1)} %fusion.100, s32[1024]{0:T(1024)S(1)} %get-tuple-element.30), kind=kCustom, calls=%fused_computation | custom fusion | bytes 12288 | tf_op jit(solution)/shard_map/gather | solution.py:191
  226.9 6.9 %gather_fusion.1 = f32[1024]{0:T(1024)S(1)} fusion(f32[512]{0:T(512)S(1)} %slice_bitcast_fusion.37, s32[1024]{0:T(1024)S(1)} %get-tuple-element.30), kind=kCustom, calls=%fused_computation.1 | custom fusion | bytes 12288 | tf_op jit(solution)/shard_map/gather | solution.py:191
  233.8 7.6 %scatter_custom_fusion = f32[512]{0:T(512)S(1)} fusion(s32[1024]{0:T(1024)S(1)} %get-tuple-element.31, f32[1024]{0:T(1024)S(1)} %get-tuple-element.86, f32[]{:T(128)} %constant.182.clone.1), kind=kCustom, calls=%fused_computation.245 | custom fusion | flops 1024 | bytes 2052 | tf_op jit(solution)/shard_map/scatter-add | solution.py:198
  241.4 7.6 %scatter_custom_fusion.1 = f32[512]{0:T(512)S(1)} fusion(s32[1024]{0:T(1024)S(1)} %get-tuple-element.31, f32[1024]{0:T(1024)S(1)} %get-tuple-element.87, f32[]{:T(128)} %constant.182.clone.1), kind=kCustom, calls=%fused_computation.243 | custom fusion | flops 1024 | bytes 2052 | tf_op jit(solution)/shard_map/scatter-add | solution.py:198
  249.2 7.8 %collective-permute-start.5 = (f32[4,4,128]{2,1,0:T(4,128)S(1)}, f32[4,4,128]{2,1,0:T(4,128)S(1)}, u32[]{:S(2)}, u32[]{:S(2)}) collective-permute-start(f32[4,4,128]{2,1,0:T(4,128)S(1)} %pad_maximum_fusion.38), channel_id=1, source_target_pairs={{32,0},{64,32},{96,64},{128,96},{160,128},{192,160},{224,192},{0,2... | collective-permute-start | bytes 24584 | tf_op jit(solution)/shard_map/ppermute | solution.py:23
  257.0 0.9 collective-permute-done.4
  258.1 2.6 collective-permute-start.6
  260.7 3.8 %collective-permute-start.7 = (f32[4,12,4]{2,1,0:T(8,128)S(1)}, f32[4,12,4]{2,1,0:T(8,128)S(1)}, u32[]{:S(2)}, u32[]{:S(2)}) collective-permute-start(f32[4,12,4]{2,1,0:T(8,128)S(1)} %get-tuple-element.49), channel_id=1, source_target_pairs={{1,0},{2,1},{3,2},{4,3},{5,4},{6,5},{7,6},{8,7},{9,8},{10,9},{11,1... | collective-permute-start | bytes 2312 | tf_op jit(solution)/shard_map/ppermute | solution.py:23
  264.5 7.6 %scatter_custom_fusion.2 = f32[512]{0:T(512)S(1)} fusion(s32[1024]{0:T(1024)S(1)} %get-tuple-element.31, f32[1024]{0:T(1024)S(1)} %get-tuple-element.26, f32[]{:T(128)} %constant.182.clone.1), kind=kCustom, calls=%fused_computation.241 | custom fusion | flops 1024 | bytes 2052 | tf_op jit(solution)/shard_map/scatter-add | solution.py:198
  273.6 17.9 %all_to_all.50 = bf16[8,3,4,128]{3,2,1,0:T(4,128)(2,1)S(1)} all-to-all(bf16[8,3,4,128]{3,2,1,0:T(4,128)(2,1)S(1)} %broadcast_in_dim.5), channel_id=1, replica_groups=mesh['grp'=8,'sp_0'=4,'sp_1'=4,'sp_2'=2] {'grp'}, dimensions={0} | all-to-all | bytes 49152 | tf_op jit(solution)/shard_map/all_to_all | solution.py:48
  291.8 20.8 %all_to_all.51 = f32[10,32,128]{2,0,1:T(8,128)S(1)} all-to-all(f32[10,32,128]{2,0,1:T(8,128)S(1)} %bitcast.180), channel_id=1, replica_groups=mesh['grp'=8,'sp_0'=4,'sp_1'=4,'sp_2'=2] {'sp_0','sp_1','sp_2'}, dimensions={1} | all-to-all | bytes 327680 | tf_op jit(solution)/shard_map/all_to_all | solution.py:173
  312.9 6.8 %fusion.51 = f32[10,512]{1,0:T(8,128)S(1)} fusion(f32[10,4096]{1,0:T(8,128)S(1)} %bitcast.173, f32[4096,256]{1,0:T(8,128)} %get-tuple-element.93, f32[4096,256]{1,0:T(8,128)} %get-tuple-element.92, f32[512]{0:T(512)S(1)} %get-tuple-element.101), kind=kOutput, calls=%fused_computation.79 | convolution fusion | flops 253760512 | bytes 8574976 | tf_op jit(solution)/shard_map/dot_general | solution.py:82
  319.7 4.1 %fusion.49 = f32[10,512]{1,0:T(8,128)S(1)} fusion(f32[10,4096]{1,0:T(8,128)S(1)} %bitcast.174, f32[4096,256]{1,0:T(8,128)S(1)} %copy-done.11, f32[4096,256]{1,0:T(8,128)S(1)} %copy-done.9, f32[512]{0:T(512)S(1)} %get-tuple-element.100), kind=kOutput, calls=%fused_computation.77 | convolution fusion | flops 253760512 | bytes 8574976 | tf_op jit(solution)/shard_map/dot_general | solution.py:82
  323.9 4.1 %fusion.47 = f32[10,512]{1,0:T(8,128)S(1)} fusion(f32[10,4096]{1,0:T(8,128)S(1)} %bitcast.175, f32[4096,256]{1,0:T(8,128)S(1)} %copy-done.15, f32[4096,256]{1,0:T(8,128)S(1)} %copy-done.13, f32[512]{0:T(512)S(1)} %get-tuple-element.99), kind=kOutput, calls=%fused_computation.75 | convolution fusion | flops 253760512 | bytes 8574976 | tf_op jit(solution)/shard_map/dot_general | solution.py:82
  327.9 4.5 %fusion.45 = f32[10,512]{1,0:T(8,128)S(1)} fusion(f32[10,4096]{1,0:T(8,128)S(1)} %bitcast.176, f32[4096,256]{1,0:T(8,128)S(1)} %copy-done.1, f32[4096,256]{1,0:T(8,128)S(1)} %copy-done.3, f32[512]{0:T(512)S(1)} %get-tuple-element.98), kind=kOutput, calls=%fused_computation.73 | convolution fusion | flops 253760512 | bytes 8574976 | tf_op jit(solution)/shard_map/dot_general | solution.py:82
  332.5 7.0 %fusion.32 = f32[10,4096]{1,0:T(8,128)S(1)} fusion(f32[10,512]{1,0:T(8,128)S(1)} %fusion.45, f32[4096,256]{1,0:T(8,128)S(1)} %copy-done.1, f32[4096,256]{1,0:T(8,128)S(1)} %copy-done.3), kind=kOutput, calls=%fused_computation.60 | convolution fusion | flops 253755392 | bytes 8572928 | tf_op jit(solution)/shard_map/dot_general | solution.py:88
  339.5 7.2 %convolution_add_fusion.2 = f32[10,4096]{1,0:T(8,128)S(1)} fusion(f32[10,4096]{1,0:T(8,128)S(1)} %fusion.32, f32[10,512]{1,0:T(8,128)S(1)} %fusion.47, f32[4096,256]{1,0:T(8,128)S(1)} %copy-done.15, f32[4096,256]{1,0:T(8,128)S(1)} %copy-done.13), kind=kOutput, calls=%fused_computation.24 | convolution fusion | flops 253796352 | bytes 8736768 | tf_op jit(solution)/shard_map/dot_general | solution.py:88
  346.7 7.0 %convolution_add_fusion.1 = f32[10,4096]{1,0:T(8,128)S(1)} fusion(f32[10,4096]{1,0:T(8,128)S(1)} %convolution_add_fusion.2, f32[10,512]{1,0:T(8,128)S(1)} %fusion.49, f32[4096,256]{1,0:T(8,128)S(1)} %copy-done.11, f32[4096,256]{1,0:T(8,128)S(1)} %copy-done.9), kind=kOutput, calls=%fused_computation.23 | convolution fusion | flops 253796352 | bytes 8736768 | tf_op jit(solution)/shard_map/dot_general | solution.py:88
  353.7 7.0 %convolution_add_fusion = f32[10,4096]{1,0:T(8,128)S(1)} fusion(f32[10,4096]{1,0:T(8,128)S(1)} %convolution_add_fusion.1, f32[10,512]{1,0:T(8,128)S(1)} %fusion.51, f32[4096,256]{1,0:T(8,128)S(1)} %copy-done.7, f32[4096,256]{1,0:T(8,128)S(1)} %copy-done.5), kind=kOutput, calls=%fused_computation.22 | convolution fusion | flops 253796352 | bytes 8736768 | tf_op jit(solution)/shard_map/dot_general | solution.py:88
  360.8 3.7 all_to_all.52
  364.7 11.2 %all_to_all.53 = f32[16,2,10,1,128]{4,1,2,3,0:T(2,128)S(1)} all-to-all(f32[16,2,10,1,128]{4,1,2,3,0:T(2,128)S(1)} %copy.33), channel_id=1, replica_groups=mesh['grp'=8,'sp_0'=4,'sp_1'=4,'sp_2'=2] {'sp_0','sp_1'}, dimensions={0} | all-to-all | bytes 327680 | tf_op jit(solution)/shard_map/all_to_all | solution.py:59
  (137 shorter events, 6.3 us)
Async XLA Ops:
  2.4 81.4 %all-to-all-start = ((f32[10,32,128]{2,0,1:T(8,128)}), f32[10,32,128]{2,0,1:T(8,128)S(1)}, u32[]{:S(2)}, u32[]{:S(2)}) async-start(f32[10,32,128]{2,0,1:T(8,128)} %copy.25), calls=%async_computation | async-start | bytes 524288 | tf_op jit(solution)/shard_map/all_to_all | solution.py:173
  12.4 17.7 %copy-start.23 = (f32[1024]{0:T(1024)S(1)}, f32[1024]{0:T(1024)}, u32[]{:S(2)}) copy-start(f32[1024]{0:T(1024)} %param.17) | copy-start | bytes 12292
  65.8 17.9 %copy-start.24 = (s32[1024]{0:T(1024)S(1)}, s32[1024]{0:T(1024)}, u32[]{:S(2)}) copy-start(s32[1024]{0:T(1024)} %param.18) | copy-start | bytes 12292
  84.1 7.5 %copy-start = (f32[4096,256]{1,0:T(8,128)S(1)}, f32[4096,256]{1,0:T(8,128)}, u32[]{:S(2)}) copy-start(f32[4096,256]{1,0:T(8,128)} %get-tuple-element.102) | copy-start | bytes 12582916
  84.1 7.5 %copy-start.2 = (f32[4096,256]{1,0:T(8,128)S(1)}, f32[4096,256]{1,0:T(8,128)}, u32[]{:S(2)}) copy-start(f32[4096,256]{1,0:T(8,128)} %get-tuple-element.103) | copy-start | bytes 12582916
  91.6 7.0 %copy-start.12 = (f32[4096,256]{1,0:T(8,128)S(1)}, f32[4096,256]{1,0:T(8,128)}, u32[]{:S(2)}) copy-start(f32[4096,256]{1,0:T(8,128)} %get-tuple-element.96) | copy-start | bytes 12582916
  91.6 7.0 %copy-start.14 = (f32[4096,256]{1,0:T(8,128)S(1)}, f32[4096,256]{1,0:T(8,128)}, u32[]{:S(2)}) copy-start(f32[4096,256]{1,0:T(8,128)} %get-tuple-element.97) | copy-start | bytes 12582916
  103.1 7.2 %copy-start.8 = (f32[4096,256]{1,0:T(8,128)S(1)}, f32[4096,256]{1,0:T(8,128)}, u32[]{:S(2)}) copy-start(f32[4096,256]{1,0:T(8,128)} %get-tuple-element.94) | copy-start | bytes 12582916
  103.1 7.2 %copy-start.10 = (f32[4096,256]{1,0:T(8,128)S(1)}, f32[4096,256]{1,0:T(8,128)}, u32[]{:S(2)}) copy-start(f32[4096,256]{1,0:T(8,128)} %get-tuple-element.95) | copy-start | bytes 12582916
  114.8 7.2 %copy-start.4 = (f32[4096,256]{1,0:T(8,128)S(1)}, f32[4096,256]{1,0:T(8,128)}, u32[]{:S(2)}) copy-start(f32[4096,256]{1,0:T(8,128)} %get-tuple-element.92) | copy-start | bytes 12582916
  114.8 7.2 %copy-start.6 = (f32[4096,256]{1,0:T(8,128)S(1)}, f32[4096,256]{1,0:T(8,128)}, u32[]{:S(2)}) copy-start(f32[4096,256]{1,0:T(8,128)} %get-tuple-element.93) | copy-start | bytes 12582916
  137.3 45.0 %copy-start.16 = (bf16[10,3,32,128]{3,2,1,0:T(8,128)(2,1)S(1)}, bf16[10,3,32,128]{3,2,1,0:T(8,128)(2,1)}, u32[]{:S(2)}) copy-start(bf16[10,3,32,128]{3,2,1,0:T(8,128)(2,1)} %param.14) | copy-start | bytes 737284
  159.8 40.5 %copy-start.18 = (f32[3,4,128]{2,1,0:T(4,128)S(1)}, f32[3,4,128]{2,1,0:T(4,128)}, u32[]{:S(2)}) copy-start(f32[3,4,128]{2,1,0:T(4,128)} %param.16) | copy-start | bytes 18436
  159.8 40.5 %copy-start.19 = (f32[3,4,128]{2,1,0:T(4,128)S(1)}, f32[3,4,128]{2,1,0:T(4,128)}, u32[]{:S(2)}) copy-start(f32[3,4,128]{2,1,0:T(4,128)} %param.15) | copy-start | bytes 18436
  162.2 15.6 %all-to-all-start.1 = ((bf16[32,2,640]{2,1,0:T(2,128)(2,1)}), bf16[32,2,640]{2,1,0:T(2,128)(2,1)S(1)}, u32[]{:S(2)}, u32[]{:S(2)}) async-start(bf16[32,2,640]{2,1,0:T(2,128)(2,1)} %reshape.241), calls=%async_computation.1 | async-start | bytes 163840 | tf_op jit(solution)/shard_map/all_to_all | solution.py:175
  183.0 17.2 %all-to-all-start.2 = ((f32[8,3,4,128]{3,2,1,0:T(4,128)}), f32[8,3,4,128]{3,2,1,0:T(4,128)S(1)}, u32[]{:S(2)}, u32[]{:S(2)}) async-start(f32[8,3,4,128]{3,2,1,0:T(4,128)} %copy.29), calls=%async_computation.2 | async-start | bytes 98304 | tf_op jit(solution)/shard_map/all_to_all | solution.py:36
  200.3 8.6 %collective-permute-start = (f32[3,4,128]{2,1,0:T(4,128)S(1)}, f32[3,4,128]{2,1,0:T(4,128)S(1)}, u32[]{:S(2)}, u32[]{:S(2)}) collective-permute-start(f32[3,4,128]{2,1,0:T(4,128)S(1)} %multiply_add_fusion.1), channel_id=1, source_target_pairs={{0,32},{32,64},{64,96},{96,128},{128,160},{160,192},{192,224},{224... | collective-permute-start | bytes 18440 | tf_op jit(solution)/shard_map/ppermute | solution.py:20
  200.6 8.2 %collective-permute-start.1 = (f32[3,4,128]{2,1,0:T(4,128)S(1)}, f32[3,4,128]{2,1,0:T(4,128)S(1)}, u32[]{:S(2)}, u32[]{:S(2)}) collective-permute-start(f32[3,4,128]{2,1,0:T(4,128)S(1)} %multiply_add_fusion.1), channel_id=1, source_target_pairs={{32,0},{64,32},{96,64},{128,96},{160,128},{192,160},{224,192},{0,2... | collective-permute-start | bytes 18440 | tf_op jit(solution)/shard_map/ppermute | solution.py:23
  208.9 10.2 %collective-permute-start.2 = (f32[3,12,4]{2,1,0:T(8,128)S(1)}, f32[3,12,4]{2,1,0:T(8,128)S(1)}, u32[]{:S(2)}, u32[]{:S(2)}) collective-permute-start(f32[3,12,4]{2,1,0:T(8,128)S(1)} %get-tuple-element.66), channel_id=1, source_target_pairs={{0,1},{1,2},{2,3},{3,4},{4,5},{5,6},{6,7},{7,8},{8,9},{9,10},{10,1... | collective-permute-start | bytes 1736 | tf_op jit(solution)/shard_map/ppermute | solution.py:20
  212.1 7.1 %collective-permute-start.3 = (f32[3,12,4]{2,1,0:T(8,128)S(1)}, f32[3,12,4]{2,1,0:T(8,128)S(1)}, u32[]{:S(2)}, u32[]{:S(2)}) collective-permute-start(f32[3,12,4]{2,1,0:T(8,128)S(1)} %get-tuple-element.67), channel_id=1, source_target_pairs={{1,0},{2,1},{3,2},{4,3},{5,4},{6,5},{7,6},{8,7},{9,8},{10,9},{11,1... | collective-permute-start | bytes 1736 | tf_op jit(solution)/shard_map/ppermute | solution.py:23
  220.0 13.8 %copy-start.20 = (f32[1024]{0:T(1024)S(1)}, f32[1024]{0:T(1024)}, u32[]{:S(2)}) copy-start(f32[1024]{0:T(1024)} %param.21) | copy-start | bytes 12292
  220.0 13.8 %copy-start.21 = (f32[1024]{0:T(1024)S(1)}, f32[1024]{0:T(1024)}, u32[]{:S(2)}) copy-start(f32[1024]{0:T(1024)} %param.20) | copy-start | bytes 12292
  220.0 13.8 %copy-start.22 = (s32[1024]{0:T(1024)S(1)}, s32[1024]{0:T(1024)}, u32[]{:S(2)}) copy-start(s32[1024]{0:T(1024)} %param.19) | copy-start | bytes 12292
  249.1 8.9 %collective-permute-start.4 = (f32[4,4,128]{2,1,0:T(4,128)S(1)}, f32[4,4,128]{2,1,0:T(4,128)S(1)}, u32[]{:S(2)}, u32[]{:S(2)}) collective-permute-start(f32[4,4,128]{2,1,0:T(4,128)S(1)} %pad_maximum_fusion.38), channel_id=1, source_target_pairs={{0,32},{32,64},{64,96},{96,128},{128,160},{160,192},{192,224},{224... | collective-permute-start | bytes 24584 | tf_op jit(solution)/shard_map/ppermute | solution.py:20
  249.2 8.8 %collective-permute-start.5 = (f32[4,4,128]{2,1,0:T(4,128)S(1)}, f32[4,4,128]{2,1,0:T(4,128)S(1)}, u32[]{:S(2)}, u32[]{:S(2)}) collective-permute-start(f32[4,4,128]{2,1,0:T(4,128)S(1)} %pad_maximum_fusion.38), channel_id=1, source_target_pairs={{32,0},{64,32},{96,64},{128,96},{160,128},{192,160},{224,192},{0,2... | collective-permute-start | bytes 24584 | tf_op jit(solution)/shard_map/ppermute | solution.py:23
  258.1 14.1 %collective-permute-start.6 = (f32[4,12,4]{2,1,0:T(8,128)S(1)}, f32[4,12,4]{2,1,0:T(8,128)S(1)}, u32[]{:S(2)}, u32[]{:S(2)}) collective-permute-start(f32[4,12,4]{2,1,0:T(8,128)S(1)} %get-tuple-element.48), channel_id=1, source_target_pairs={{0,1},{1,2},{2,3},{3,4},{4,5},{5,6},{6,7},{7,8},{8,9},{9,10},{10,1... | collective-permute-start | bytes 2312 | tf_op jit(solution)/shard_map/ppermute | solution.py:20
  260.7 11.5 %collective-permute-start.7 = (f32[4,12,4]{2,1,0:T(8,128)S(1)}, f32[4,12,4]{2,1,0:T(8,128)S(1)}, u32[]{:S(2)}, u32[]{:S(2)}) collective-permute-start(f32[4,12,4]{2,1,0:T(8,128)S(1)} %get-tuple-element.49), channel_id=1, source_target_pairs={{1,0},{2,1},{3,2},{4,3},{5,4},{6,5},{7,6},{8,7},{9,8},{10,9},{11,1... | collective-permute-start | bytes 2312 | tf_op jit(solution)/shard_map/ppermute | solution.py:23
  312.8 6.9 %copy-start.9 = (f32[4096,256]{1,0:T(8,128)S(1)}, f32[4096,256]{1,0:T(8,128)}, u32[]{:S(2)}) copy-start(f32[4096,256]{1,0:T(8,128)} %get-tuple-element.94) | copy-start | bytes 12582916
  312.9 6.9 %copy-start.11 = (f32[4096,256]{1,0:T(8,128)S(1)}, f32[4096,256]{1,0:T(8,128)}, u32[]{:S(2)}) copy-start(f32[4096,256]{1,0:T(8,128)} %get-tuple-element.95) | copy-start | bytes 12582916
  319.7 4.1 %copy-start.13 = (f32[4096,256]{1,0:T(8,128)S(1)}, f32[4096,256]{1,0:T(8,128)}, u32[]{:S(2)}) copy-start(f32[4096,256]{1,0:T(8,128)} %get-tuple-element.96) | copy-start | bytes 12582916
  319.7 4.1 %copy-start.15 = (f32[4096,256]{1,0:T(8,128)S(1)}, f32[4096,256]{1,0:T(8,128)}, u32[]{:S(2)}) copy-start(f32[4096,256]{1,0:T(8,128)} %get-tuple-element.97) | copy-start | bytes 12582916
  323.8 4.1 %copy-start.1 = (f32[4096,256]{1,0:T(8,128)S(1)}, f32[4096,256]{1,0:T(8,128)}, u32[]{:S(2)}) copy-start(f32[4096,256]{1,0:T(8,128)} %get-tuple-element.102) | copy-start | bytes 12582916
  323.8 4.1 %copy-start.3 = (f32[4096,256]{1,0:T(8,128)S(1)}, f32[4096,256]{1,0:T(8,128)}, u32[]{:S(2)}) copy-start(f32[4096,256]{1,0:T(8,128)} %get-tuple-element.103) | copy-start | bytes 12582916
  346.6 7.0 %copy-start.5 = (f32[4096,256]{1,0:T(8,128)S(1)}, f32[4096,256]{1,0:T(8,128)}, u32[]{:S(2)}) copy-start(f32[4096,256]{1,0:T(8,128)} %get-tuple-element.92) | copy-start | bytes 12582916
  346.7 7.0 %copy-start.7 = (f32[4096,256]{1,0:T(8,128)S(1)}, f32[4096,256]{1,0:T(8,128)}, u32[]{:S(2)}) copy-start(f32[4096,256]{1,0:T(8,128)} %get-tuple-element.93) | copy-start | bytes 12582916
  353.7 22.4 %copy-start.17 = (f32[10,32,128]{2,1,0:T(8,128)S(1)}, f32[10,32,128]{2,1,0:T(8,128)}, u32[]{:S(2)}) copy-start(f32[10,32,128]{2,1,0:T(8,128)} %param.13) | copy-start | bytes 491524
where the time goes:
time: 383 us; the launch traced here: 377 us
  other arithmetic  120 us (31%)
  matrix products  97.4 us (25%)
  blocking collectives  53.7 us (14%)
  starting transfers between devices  51.1 us (13%)
  local copies, waits for them, and re-layouts  34.5 us (9%)
  waiting for transfers between devices  18.9 us (5%)
    dot_general x8, matrix products, spectral_filter(): jnp.dot(coeffs * weights[None, :], fourier_basis.T, precision=lax.Precisi...  56.9 us
    cos x3, other arithmetic, spectral_filter(): jnp.cos(radians)  53.6 us
    dot_general x8, matrix products, spectral_filter(): jnp.dot(rows_data, fourier_basis, precision=lax.Precision.HIGHEST, prefer...  40.5 us
    scatter-add x3, other arithmetic, per_device(): jnp.zeros((tile_rows * tile_cols,), jnp.float32).at[local_index]  22.8 us
    unnamed x4, other arithmetic  22.5 us
    all_to_all x1, blocking collectives, to_rows(): lax.all_to_all(columns, SP, split_axis=1, concat_axis=2, tiled=True)  20.8 us
    gather x3, local copies, waits for them, and re-layouts, per_device(): values = states[moment][0].reshape(-1)[local_index]  20.6 us
    ppermute x4, starting transfers between devices, extended(): lax.ppermute(lax.slice_in_dim(block, 0, width, axis=dim), axis, backward)  19 us
  transfers between devices with their start and end apart: 11, of which 4 were waited for; matrix products, arithmetic and copies ran while one was open for 23% of the time, Pallas kernels for 0%

commit v1 on v0

--- a/solution.py
+++ b/solution.py
@@ -172,9 +172,11 @@
     def to_rows(columns):
         return localize_items(lax.all_to_all(columns, SP, split_axis=1, concat_axis=2, tiled=True))
 
-    localized = lax.all_to_all(
-        to_rows(alpha).astype(jnp.bfloat16), SP, split_axis=2, concat_axis=1, tiled=True
-    )
+    value = to_rows(alpha).astype(jnp.bfloat16)
+    count_2 = lax.axis_size(SP)
+    blocks = jnp.stack(jnp.split(value, count_2, axis=2), axis=0)
+    blocks = lax.all_to_all(blocks, SP, split_axis=0, concat_axis=0)
+    localized = jnp.concatenate(blocks, axis=1)
     partial_value = jnp.einsum(
         "mvyx,myx->vyx", ensemble, localized, preferred_element_type=jnp.float32
     )

time: 383 us -> 369 us (0.963)
  other arithmetic: 120 us -> 97.2 us
  waiting for transfers between devices: 18.9 us -> 33.1 us
  starting transfers between devices: 51.1 us -> 38.8 us
  local copies, waits for them, and re-layouts: 34.5 us -> 43.4 us
    unnamed x4 -> x3, other arithmetic: 22.5 us -> 0.08 us
    ppermute x4, starting transfers between devices: 19 us -> 5.29 us  [extended(): lax.ppermute(lax.slice_in_dim(block, 0, width, axis=dim), axis, backward)]
    unnamed x60 -> x88, local copies, waits for them, and re-layouts: 7.55 us -> 20.8 us
    ppermute x4, waiting for transfers between devices: 1.96 us -> 13.4 us  [extended(): lax.ppermute(lax.slice_in_dim(block, block.shape[dim] - width, None, axis...]
  transfers between devices with their start and end apart: 11 -> 11, of which waited for: 4 -> 6; matrix products, arithmetic and copies ran while one was open for 23% -> 24% of each run, Pallas kernels for 0% -> 0%
where the time goes in v1:
time: 369 us; the launch traced here: 362 us
  matrix products  97.3 us (26%)
  other arithmetic  97.2 us (26%)
  blocking collectives  50.8 us (14%)
  local copies, waits for them, and re-layouts  43.4 us (12%)
  starting transfers between devices  38.8 us (11%)
  waiting for transfers between devices  33.1 us (9%)
    dot_general x8, matrix products, spectral_filter(): jnp.dot(coeffs * weights[None, :], fourier_basis.T, precision=lax.Precisi...  56.9 us
    cos x3, other arithmetic, spectral_filter(): jnp.cos(radians)  53.6 us
    dot_general x8, matrix products, spectral_filter(): jnp.dot(rows_data, fourier_basis, precision=lax.Precision.HIGHEST, prefer...  40.4 us
    scatter-add x3, other arithmetic, per_device(): jnp.zeros((tile_rows * tile_cols,), jnp.float32).at[local_index]  22.8 us
    all_to_all x1, blocking collectives, to_rows(): lax.all_to_all(columns, SP, split_axis=1, concat_axis=2, tiled=True)  20.8 us
    unnamed x88, local copies, waits for them, and re-layouts  20.8 us
    gather x3, local copies, waits for them, and re-layouts, per_device(): values = states[moment][0].reshape(-1)[local_index]  20.6 us
    sin x1, other arithmetic, spectral_filter(): jnp.sin(radians)  17.6 us
  transfers between devices with their start and end apart: 11, of which 6 were waited for; matrix products, arithmetic and copies ran while one was open for 24% of the time, Pallas kernels for 0%

profile of v1, /device:TPU:1, one launch (start us, length us, event | category | flops | bytes accessed | tf_op | source)
XLA Modules:
  0.0 362.3 jit_solution(2236273542922296528)
XLA Ops:
  0.6 1.7 copy.22
  2.4 10.0 %all-to-all-start = ((f32[10,32,128]{2,0,1:T(8,128)}), f32[10,32,128]{2,0,1:T(8,128)S(1)}, u32[]{:S(2)}, u32[]{:S(2)}) async-start(f32[10,32,128]{2,0,1:T(8,128)} %copy.22), calls=%async_computation | async-start | bytes 524288 | tf_op jit(solution)/shard_map/all_to_all | solution.py:173
  12.5 17.6 %fusion.36 = (f32[4096,256]{1,0:T(8,128)}, f32[4096,256]{1,0:T(8,128)}) fusion(), kind=kLoop, calls=%fused_computation.64 | loop fusion | flops 14680064 | bytes 8388608 | tf_op jit(solution)/shard_map/sin | solution.py:79
  30.1 17.9 %fusion.39 = (f32[4096,256]{1,0:T(8,128)}, f32[4096,256]{1,0:T(8,128)}) fusion(s32[256]{0:T(256)S(1)} %iota_add_fusion), kind=kLoop, calls=%fused_computation.67 | loop fusion | flops 14680064 | bytes 8389632 | tf_op jit(solution)/shard_map/cos | solution.py:79
  47.9 17.9 %fusion.41 = (f32[4096,256]{1,0:T(8,128)}, f32[4096,256]{1,0:T(8,128)}) fusion(s32[256]{0:T(256)S(1)} %iota_add_fusion.1), kind=kLoop, calls=%fused_computation.69 | loop fusion | flops 14680064 | bytes 8389632 | tf_op jit(solution)/shard_map/cos | solution.py:79
  65.8 17.9 %fusion.43 = (f32[4096,256]{1,0:T(8,128)}, f32[4096,256]{1,0:T(8,128)}) fusion(s32[256]{0:T(256)S(1)} %iota_add_fusion.2), kind=kLoop, calls=%fused_computation.71 | loop fusion | flops 14680064 | bytes 8389632 | tf_op jit(solution)/shard_map/cos | solution.py:79
  84.1 7.5 %fusion.44 = f32[512,10]{0,1:T(8,128)S(1)} fusion(f32[10,4096]{1,0:T(8,128)S(1)} %bitcast.305, f32[4096,256]{1,0:T(8,128)} %get-tuple-element.102, f32[4096,256]{1,0:T(8,128)} %get-tuple-element.103, f32[512]{0:T(512)S(1)} %get-tuple-element.98), kind=kOutput, calls=%fused_computation.72 | convolution fusion | flops 253760512 | bytes 8574976 | tf_op jit(solution)/shard_map/dot_general | solution.py:82
  91.6 7.0 %fusion.34 = f32[10,4096]{1,0:T(8,128)S(1)} fusion(f32[512,10]{0,1:T(8,128)S(1)} %fusion.44, f32[4096,256]{1,0:T(8,128)S(1)} %copy-done, f32[4096,256]{1,0:T(8,128)S(1)} %copy-done.2), kind=kOutput, calls=%fused_computation.62 | convolution fusion | flops 253755392 | bytes 8572928 | tf_op jit(solution)/shard_map/dot_general | solution.py:88
  98.6 4.5 %fusion.46 = f32[512,10]{0,1:T(8,128)S(1)} fusion(f32[10,4096]{1,0:T(8,128)S(1)} %bitcast.306, f32[4096,256]{1,0:T(8,128)S(1)} %copy-done.14, f32[4096,256]{1,0:T(8,128)S(1)} %copy-done.12, f32[512]{0:T(512)S(1)} %get-tuple-element.99), kind=kOutput, calls=%fused_computation.74 | convolution fusion | flops 253760512 | bytes 8574976 | tf_op jit(solution)/shard_map/dot_general | solution.py:82
  103.1 7.2 %convolution_add_fusion.5 = f32[10,4096]{1,0:T(8,128)S(1)} fusion(f32[10,4096]{1,0:T(8,128)S(1)} %fusion.34, f32[512,10]{0,1:T(8,128)S(1)} %fusion.46, f32[4096,256]{1,0:T(8,128)S(1)} %copy-done.14, f32[4096,256]{1,0:T(8,128)S(1)} %copy-done.12), kind=kOutput, calls=%fused_computation.27 | convolution fusion | flops 253796352 | bytes 8736768 | tf_op jit(solution)/shard_map/dot_general | solution.py:88
  110.3 4.5 %fusion.48 = f32[512,10]{0,1:T(8,128)S(1)} fusion(f32[10,4096]{1,0:T(8,128)S(1)} %bitcast.307, f32[4096,256]{1,0:T(8,128)S(1)} %copy-done.10, f32[4096,256]{1,0:T(8,128)S(1)} %copy-done.8, f32[512]{0:T(512)S(1)} %get-tuple-element.100), kind=kOutput, calls=%fused_computation.76 | convolution fusion | flops 253760512 | bytes 8574976 | tf_op jit(solution)/shard_map/dot_general | solution.py:82
  114.8 7.4 %convolution_add_fusion.4 = f32[10,4096]{1,0:T(8,128)S(1)} fusion(f32[10,4096]{1,0:T(8,128)S(1)} %convolution_add_fusion.5, f32[512,10]{0,1:T(8,128)S(1)} %fusion.48, f32[4096,256]{1,0:T(8,128)S(1)} %copy-done.10, f32[4096,256]{1,0:T(8,128)S(1)} %copy-done.8), kind=kOutput, calls=%fused_computation.26 | convolution fusion | flops 253796352 | bytes 8736768 | tf_op jit(solution)/shard_map/dot_general | solution.py:88
  122.3 4.5 %fusion.50 = f32[512,10]{0,1:T(8,128)S(1)} fusion(f32[10,4096]{1,0:T(8,128)S(1)} %bitcast.308, f32[4096,256]{1,0:T(8,128)S(1)} %copy-done.6, f32[4096,256]{1,0:T(8,128)S(1)} %copy-done.4, f32[512]{0:T(512)S(1)} %get-tuple-element.101), kind=kOutput, calls=%fused_computation.78 | convolution fusion | flops 253760512 | bytes 8574976 | tf_op jit(solution)/shard_map/dot_general | solution.py:82
  126.8 7.2 %fusion.1 = bf16[10,1,4096]{2,0,1:T(8,128)(2,1)S(1)} fusion(f32[10,4096]{1,0:T(8,128)S(1)} %convolution_add_fusion.4, f32[512,10]{0,1:T(8,128)S(1)} %fusion.50, f32[4096,256]{1,0:T(8,128)S(1)} %copy-done.6, f32[4096,256]{1,0:T(8,128)S(1)} %copy-done.4), kind=kOutput, calls=%fused_computation.29 | convolution fusion | flops 253837312 | bytes 8654848 | tf_op jit(solution)/shard_map/dot_general | solution.py:88
  133.9 0.6 constant_dynamic-update-slice_fusion.31
  153.0 7.7 %all-to-all-start.1 = ((bf16[32,10,1,128]{3,1,2,0:T(8,128)(2,1)}), bf16[32,10,1,128]{3,1,2,0:T(8,128)(2,1)S(1)}, u32[]{:S(2)}, u32[]{:S(2)}) async-start(bf16[32,10,1,128]{3,1,2,0:T(8,128)(2,1)} %constant_dynamic-update-slice_fusion), calls=%async_computation.1 | async-start | bytes 262144 | tf_op jit(solution)/shard_map/all_to_all | solution.py:178
  160.8 8.5 %all-to-all-done.1 = bf16[32,10,1,128]{3,1,2,0:T(8,128)(2,1)S(1)} async-done(((bf16[32,10,1,128]{3,1,2,0:T(8,128)(2,1)}), bf16[32,10,1,128]{3,1,2,0:T(8,128)(2,1)S(1)}, u32[]{:S(2)}, u32[]{:S(2)}) %all-to-all-start.1) | async-done | bytes 81952 | tf_op jit(solution)/shard_map/all_to_all | solution.py:178
  169.5 0.6 copy.24
  170.1 8.1 %all-to-all-start.2 = ((f32[8,3,4,128]{3,2,1,0:T(4,128)}), f32[8,3,4,128]{3,2,1,0:T(4,128)S(1)}, u32[]{:S(2)}, u32[]{:S(2)}) async-start(f32[8,3,4,128]{3,2,1,0:T(4,128)} %copy.24), calls=%async_computation.2 | async-start | bytes 98304 | tf_op jit(solution)/shard_map/all_to_all | solution.py:36
  178.2 9.1 %all-to-all-done.2 = f32[8,3,4,128]{3,2,1,0:T(4,128)S(1)} async-done(((f32[8,3,4,128]{3,2,1,0:T(4,128)}), f32[8,3,4,128]{3,2,1,0:T(4,128)S(1)}, u32[]{:S(2)}, u32[]{:S(2)}) %all-to-all-start.2) | async-done | bytes 49184 | tf_op jit(solution)/shard_map/all_to_all | solution.py:36
  187.3 1.4 collective-permute-start.1
  188.9 1.0 collective-permute-done.1
  189.9 7.3 %collective-permute-done = f32[3,4,128]{2,1,0:T(4,128)S(1)} collective-permute-done((f32[3,4,128]{2,1,0:T(4,128)S(1)}, f32[3,4,128]{2,1,0:T(4,128)S(1)}, u32[]{:S(2)}, u32[]{:S(2)}) %collective-permute-start) | collective-permute-done | bytes 6176 | tf_op jit(solution)/shard_map/ppermute | solution.py:20
  197.3 3.2 collective-permute-start.2
  200.5 6.9 %gather_fusion.2 = f32[1024]{0:T(1024)S(1)} fusion(f32[512]{0:T(512)S(1)} %slice_bitcast_fusion.67, s32[1024]{0:T(1024)S(1)} %get-tuple-element.30), kind=kCustom, calls=%fused_computation.2 | custom fusion | bytes 12288 | tf_op jit(solution)/shard_map/gather | solution.py:193
  208.2 6.9 %gather_fusion = f32[1024]{0:T(1024)S(1)} fusion(f32[512]{0:T(512)S(1)} %fusion.99, s32[1024]{0:T(1024)S(1)} %get-tuple-element.30), kind=kCustom, calls=%fused_computation | custom fusion | bytes 12288 | tf_op jit(solution)/shard_map/gather | solution.py:193
  215.1 6.9 %gather_fusion.1 = f32[1024]{0:T(1024)S(1)} fusion(f32[512]{0:T(512)S(1)} %slice_bitcast_fusion.68, s32[1024]{0:T(1024)S(1)} %get-tuple-element.30), kind=kCustom, calls=%fused_computation.1 | custom fusion | bytes 12288 | tf_op jit(solution)/shard_map/gather | solution.py:193
  222.0 7.6 %scatter_custom_fusion = f32[512]{0:T(512)S(1)} fusion(s32[1024]{0:T(1024)S(1)} %get-tuple-element.31, f32[1024]{0:T(1024)S(1)} %get-tuple-element.86, f32[]{:T(128)} %constant.182.clone.1), kind=kCustom, calls=%fused_computation.308 | custom fusion | flops 1024 | bytes 2052 | tf_op jit(solution)/shard_map/scatter-add | solution.py:200
  229.6 7.6 %scatter_custom_fusion.1 = f32[512]{0:T(512)S(1)} fusion(s32[1024]{0:T(1024)S(1)} %get-tuple-element.31, f32[1024]{0:T(1024)S(1)} %get-tuple-element.87, f32[]{:T(128)} %constant.182.clone.1), kind=kCustom, calls=%fused_computation.306 | custom fusion | flops 1024 | bytes 2052 | tf_op jit(solution)/shard_map/scatter-add | solution.py:200
  237.4 1.5 collective-permute-start.4
  238.8 1.0 collective-permute-done.5
  239.9 6.1 %collective-permute-done.4 = f32[4,4,128]{2,1,0:T(4,128)S(1)} collective-permute-done((f32[4,4,128]{2,1,0:T(4,128)S(1)}, f32[4,4,128]{2,1,0:T(4,128)S(1)}, u32[]{:S(2)}, u32[]{:S(2)}) %collective-permute-start.4) | collective-permute-done | bytes 8224 | tf_op jit(solution)/shard_map/ppermute | solution.py:20
  246.1 2.9 collective-permute-start.6
  249.0 3.8 %collective-permute-start.7 = (f32[4,12,4]{2,1,0:T(8,128)S(1)}, f32[4,12,4]{2,1,0:T(8,128)S(1)}, u32[]{:S(2)}, u32[]{:S(2)}) collective-permute-start(f32[4,12,4]{2,1,0:T(8,128)S(1)} %get-tuple-element.49), channel_id=1, source_target_pairs={{1,0},{2,1},{3,2},{4,3},{5,4},{6,5},{7,6},{8,7},{9,8},{10,9},{11,1... | collective-permute-start | bytes 2312 | tf_op jit(solution)/shard_map/ppermute | solution.py:23
  252.8 7.6 %scatter_custom_fusion.2 = f32[512]{0:T(512)S(1)} fusion(s32[1024]{0:T(1024)S(1)} %get-tuple-element.31, f32[1024]{0:T(1024)S(1)} %get-tuple-element.26, f32[]{:T(128)} %constant.182.clone.1), kind=kCustom, calls=%fused_computation.304 | custom fusion | flops 1024 | bytes 2052 | tf_op jit(solution)/shard_map/scatter-add | solution.py:200
  261.9 15.0 %all_to_all.43 = bf16[8,3,4,128]{3,2,1,0:T(4,128)(2,1)S(1)} all-to-all(bf16[8,3,4,128]{3,2,1,0:T(4,128)(2,1)S(1)} %broadcast_in_dim.5), channel_id=1, replica_groups=mesh['grp'=8,'sp_0'=4,'sp_1'=4,'sp_2'=2] {'grp'}, dimensions={0} | all-to-all | bytes 49152 | tf_op jit(solution)/shard_map/all_to_all | solution.py:48
  277.1 20.8 %all_to_all.44 = f32[10,32,128]{2,0,1:T(8,128)S(1)} all-to-all(f32[10,32,128]{2,0,1:T(8,128)S(1)} %bitcast.301), channel_id=1, replica_groups=mesh['grp'=8,'sp_0'=4,'sp_1'=4,'sp_2'=2] {'sp_0','sp_1','sp_2'}, dimensions={1} | all-to-all | bytes 327680 | tf_op jit(solution)/shard_map/all_to_all | solution.py:173
  298.3 7.0 %fusion.51 = f32[10,512]{1,0:T(8,128)S(1)} fusion(f32[10,4096]{1,0:T(8,128)S(1)} %bitcast.294, f32[4096,256]{1,0:T(8,128)} %get-tuple-element.93, f32[4096,256]{1,0:T(8,128)} %get-tuple-element.92, f32[512]{0:T(512)S(1)} %get-tuple-element.101), kind=kOutput, calls=%fused_computation.79 | convolution fusion | flops 253760512 | bytes 8574976 | tf_op jit(solution)/shard_map/dot_general | solution.py:82
  305.3 4.1 %fusion.49 = f32[10,512]{1,0:T(8,128)S(1)} fusion(f32[10,4096]{1,0:T(8,128)S(1)} %bitcast.295, f32[4096,256]{1,0:T(8,128)S(1)} %copy-done.11, f32[4096,256]{1,0:T(8,128)S(1)} %copy-done.9, f32[512]{0:T(512)S(1)} %get-tuple-element.100), kind=kOutput, calls=%fused_computation.77 | convolution fusion | flops 253760512 | bytes 8574976 | tf_op jit(solution)/shard_map/dot_general | solution.py:82
  309.4 4.1 %fusion.47 = f32[10,512]{1,0:T(8,128)S(1)} fusion(f32[10,4096]{1,0:T(8,128)S(1)} %bitcast.296, f32[4096,256]{1,0:T(8,128)S(1)} %copy-done.15, f32[4096,256]{1,0:T(8,128)S(1)} %copy-done.13, f32[512]{0:T(512)S(1)} %get-tuple-element.99), kind=kOutput, calls=%fused_computation.75 | convolution fusion | flops 253760512 | bytes 8574976 | tf_op jit(solution)/shard_map/dot_general | solution.py:82
  313.5 4.3 %fusion.45 = f32[10,512]{1,0:T(8,128)S(1)} fusion(f32[10,4096]{1,0:T(8,128)S(1)} %bitcast.297, f32[4096,256]{1,0:T(8,128)S(1)} %copy-done.1, f32[4096,256]{1,0:T(8,128)S(1)} %copy-done.3, f32[512]{0:T(512)S(1)} %get-tuple-element.98), kind=kOutput, calls=%fused_computation.73 | convolution fusion | flops 253760512 | bytes 8574976 | tf_op jit(solution)/shard_map/dot_general | solution.py:82
  317.8 7.0 %fusion.32 = f32[10,4096]{1,0:T(8,128)S(1)} fusion(f32[10,512]{1,0:T(8,128)S(1)} %fusion.45, f32[4096,256]{1,0:T(8,128)S(1)} %copy-done.1, f32[4096,256]{1,0:T(8,128)S(1)} %copy-done.3), kind=kOutput, calls=%fused_computation.60 | convolution fusion | flops 253755392 | bytes 8572928 | tf_op jit(solution)/shard_map/dot_general | solution.py:88
  324.8 7.2 %convolution_add_fusion.2 = f32[10,4096]{1,0:T(8,128)S(1)} fusion(f32[10,4096]{1,0:T(8,128)S(1)} %fusion.32, f32[10,512]{1,0:T(8,128)S(1)} %fusion.47, f32[4096,256]{1,0:T(8,128)S(1)} %copy-done.15, f32[4096,256]{1,0:T(8,128)S(1)} %copy-done.13), kind=kOutput, calls=%fused_computation.24 | convolution fusion | flops 253796352 | bytes 8736768 | tf_op jit(solution)/shard_map/dot_general | solution.py:88
  332.0 7.0 %convolution_add_fusion.1 = f32[10,4096]{1,0:T(8,128)S(1)} fusion(f32[10,4096]{1,0:T(8,128)S(1)} %convolution_add_fusion.2, f32[10,512]{1,0:T(8,128)S(1)} %fusion.49, f32[4096,256]{1,0:T(8,128)S(1)} %copy-done.11, f32[4096,256]{1,0:T(8,128)S(1)} %copy-done.9), kind=kOutput, calls=%fused_computation.23 | convolution fusion | flops 253796352 | bytes 8736768 | tf_op jit(solution)/shard_map/dot_general | solution.py:88
  339.0 7.0 %convolution_add_fusion = f32[10,4096]{1,0:T(8,128)S(1)} fusion(f32[10,4096]{1,0:T(8,128)S(1)} %convolution_add_fusion.1, f32[10,512]{1,0:T(8,128)S(1)} %fusion.51, f32[4096,256]{1,0:T(8,128)S(1)} %copy-done.7, f32[4096,256]{1,0:T(8,128)S(1)} %copy-done.5), kind=kOutput, calls=%fused_computation.22 | convolution fusion | flops 253796352 | bytes 8736768 | tf_op jit(solution)/shard_map/dot_general | solution.py:88
  346.1 3.7 %all_to_all.45 = f32[16,2,10,1,128]{4,0,2,3,1:T(8,128)S(1)} all-to-all(f32[16,2,10,1,128]{4,0,2,3,1:T(8,128)S(1)} %copy.27), channel_id=1, replica_groups=mesh['grp'=8,'sp_0'=4,'sp_1'=4,'sp_2'=2] {'sp_2'}, dimensions={1} | all-to-all | bytes 327680 | tf_op jit(solution)/shard_map/all_to_all | solution.py:59
  350.0 11.2 %all_to_all.46 = f32[16,2,10,1,128]{4,1,2,3,0:T(2,128)S(1)} all-to-all(f32[16,2,10,1,128]{4,1,2,3,0:T(2,128)S(1)} %copy.28), channel_id=1, replica_groups=mesh['grp'=8,'sp_0'=4,'sp_1'=4,'sp_2'=2] {'sp_0','sp_1'}, dimensions={0} | all-to-all | bytes 327680 | tf_op jit(solution)/shard_map/all_to_all | solution.py:59
  361.4 0.7 add.330
  (163 shorter events, 22.6 us)
Async XLA Ops:
  2.4 81.4 %all-to-all-start = ((f32[10,32,128]{2,0,1:T(8,128)}), f32[10,32,128]{2,0,1:T(8,128)S(1)}, u32[]{:S(2)}, u32[]{:S(2)}) async-start(f32[10,32,128]{2,0,1:T(8,128)} %copy.22), calls=%async_computation | async-start | bytes 524288 | tf_op jit(solution)/shard_map/all_to_all | solution.py:173
  12.5 17.6 %copy-start.23 = (f32[1024]{0:T(1024)S(1)}, f32[1024]{0:T(1024)}, u32[]{:S(2)}) copy-start(f32[1024]{0:T(1024)} %param.17) | copy-start | bytes 12292
  65.8 17.9 %copy-start.24 = (s32[1024]{0:T(1024)S(1)}, s32[1024]{0:T(1024)}, u32[]{:S(2)}) copy-start(s32[1024]{0:T(1024)} %param.18) | copy-start | bytes 12292
  84.0 7.5 %copy-start = (f32[4096,256]{1,0:T(8,128)S(1)}, f32[4096,256]{1,0:T(8,128)}, u32[]{:S(2)}) copy-start(f32[4096,256]{1,0:T(8,128)} %get-tuple-element.102) | copy-start | bytes 12582916
  84.0 7.5 %copy-start.2 = (f32[4096,256]{1,0:T(8,128)S(1)}, f32[4096,256]{1,0:T(8,128)}, u32[]{:S(2)}) copy-start(f32[4096,256]{1,0:T(8,128)} %get-tuple-element.103) | copy-start | bytes 12582916
  91.6 7.0 %copy-start.12 = (f32[4096,256]{1,0:T(8,128)S(1)}, f32[4096,256]{1,0:T(8,128)}, u32[]{:S(2)}) copy-start(f32[4096,256]{1,0:T(8,128)} %get-tuple-element.96) | copy-start | bytes 12582916
  91.6 7.0 %copy-start.14 = (f32[4096,256]{1,0:T(8,128)S(1)}, f32[4096,256]{1,0:T(8,128)}, u32[]{:S(2)}) copy-start(f32[4096,256]{1,0:T(8,128)} %get-tuple-element.97) | copy-start | bytes 12582916
  103.1 7.2 %copy-start.8 = (f32[4096,256]{1,0:T(8,128)S(1)}, f32[4096,256]{1,0:T(8,128)}, u32[]{:S(2)}) copy-start(f32[4096,256]{1,0:T(8,128)} %get-tuple-element.94) | copy-start | bytes 12582916
  103.1 7.2 %copy-start.10 = (f32[4096,256]{1,0:T(8,128)S(1)}, f32[4096,256]{1,0:T(8,128)}, u32[]{:S(2)}) copy-start(f32[4096,256]{1,0:T(8,128)} %get-tuple-element.95) | copy-start | bytes 12582916
  114.8 7.4 %copy-start.4 = (f32[4096,256]{1,0:T(8,128)S(1)}, f32[4096,256]{1,0:T(8,128)}, u32[]{:S(2)}) copy-start(f32[4096,256]{1,0:T(8,128)} %get-tuple-element.92) | copy-start | bytes 12582916
  114.8 7.4 %copy-start.6 = (f32[4096,256]{1,0:T(8,128)S(1)}, f32[4096,256]{1,0:T(8,128)}, u32[]{:S(2)}) copy-start(f32[4096,256]{1,0:T(8,128)} %get-tuple-element.93) | copy-start | bytes 12582916
  126.7 42.6 %copy-start.16 = (bf16[10,3,32,128]{3,2,1,0:T(8,128)(2,1)S(1)}, bf16[10,3,32,128]{3,2,1,0:T(8,128)(2,1)}, u32[]{:S(2)}) copy-start(bf16[10,3,32,128]{3,2,1,0:T(8,128)(2,1)} %param.14) | copy-start | bytes 737284
  126.8 60.5 %copy-start.18 = (f32[3,4,128]{2,1,0:T(4,128)S(1)}, f32[3,4,128]{2,1,0:T(4,128)}, u32[]{:S(2)}) copy-start(f32[3,4,128]{2,1,0:T(4,128)} %param.16) | copy-start | bytes 18436
  126.8 60.5 %copy-start.19 = (f32[3,4,128]{2,1,0:T(4,128)S(1)}, f32[3,4,128]{2,1,0:T(4,128)}, u32[]{:S(2)}) copy-start(f32[3,4,128]{2,1,0:T(4,128)} %param.15) | copy-start | bytes 18436
  153.0 16.3 %all-to-all-start.1 = ((bf16[32,10,1,128]{3,1,2,0:T(8,128)(2,1)}), bf16[32,10,1,128]{3,1,2,0:T(8,128)(2,1)S(1)}, u32[]{:S(2)}, u32[]{:S(2)}) async-start(bf16[32,10,1,128]{3,1,2,0:T(8,128)(2,1)} %constant_dynamic-update-slice_fusion), calls=%async_computation.1 | async-start | bytes 262144 | tf_op jit(solution)/shard_map/all_to_all | solution.py:178
  170.1 17.2 %all-to-all-start.2 = ((f32[8,3,4,128]{3,2,1,0:T(4,128)}), f32[8,3,4,128]{3,2,1,0:T(4,128)S(1)}, u32[]{:S(2)}, u32[]{:S(2)}) async-start(f32[8,3,4,128]{3,2,1,0:T(4,128)} %copy.24), calls=%async_computation.2 | async-start | bytes 98304 | tf_op jit(solution)/shard_map/all_to_all | solution.py:36
  187.3 2.6 collective-permute-start.1
  188.7 8.5 %collective-permute-start = (f32[3,4,128]{2,1,0:T(4,128)S(1)}, f32[3,4,128]{2,1,0:T(4,128)S(1)}, u32[]{:S(2)}, u32[]{:S(2)}) collective-permute-start(f32[3,4,128]{2,1,0:T(4,128)S(1)} %multiply_add_fusion.1), channel_id=1, source_target_pairs={{0,32},{32,64},{64,96},{96,128},{128,160},{160,192},{192,224},{224... | collective-permute-start | bytes 18440 | tf_op jit(solution)/shard_map/ppermute | solution.py:20
  197.3 10.0 %collective-permute-start.2 = (f32[3,12,4]{2,1,0:T(8,128)S(1)}, f32[3,12,4]{2,1,0:T(8,128)S(1)}, u32[]{:S(2)}, u32[]{:S(2)}) collective-permute-start(f32[3,12,4]{2,1,0:T(8,128)S(1)} %get-tuple-element.66), channel_id=1, source_target_pairs={{0,1},{1,2},{2,3},{3,4},{4,5},{5,6},{6,7},{7,8},{8,9},{9,10},{10,1... | collective-permute-start | bytes 1736 | tf_op jit(solution)/shard_map/ppermute | solution.py:20
  200.4 6.9 %collective-permute-start.3 = (f32[3,12,4]{2,1,0:T(8,128)S(1)}, f32[3,12,4]{2,1,0:T(8,128)S(1)}, u32[]{:S(2)}, u32[]{:S(2)}) collective-permute-start(f32[3,12,4]{2,1,0:T(8,128)S(1)} %get-tuple-element.67), channel_id=1, source_target_pairs={{1,0},{2,1},{3,2},{4,3},{5,4},{6,5},{7,6},{8,7},{9,8},{10,9},{11,1... | collective-permute-start | bytes 1736 | tf_op jit(solution)/shard_map/ppermute | solution.py:23
  208.2 13.8 %copy-start.20 = (f32[1024]{0:T(1024)S(1)}, f32[1024]{0:T(1024)}, u32[]{:S(2)}) copy-start(f32[1024]{0:T(1024)} %param.21) | copy-start | bytes 12292
  208.2 13.8 %copy-start.21 = (f32[1024]{0:T(1024)S(1)}, f32[1024]{0:T(1024)}, u32[]{:S(2)}) copy-start(f32[1024]{0:T(1024)} %param.20) | copy-start | bytes 12292
  208.2 13.8 %copy-start.22 = (s32[1024]{0:T(1024)S(1)}, s32[1024]{0:T(1024)}, u32[]{:S(2)}) copy-start(s32[1024]{0:T(1024)} %param.19) | copy-start | bytes 12292
  237.3 2.6 collective-permute-start.5
  237.4 8.6 %collective-permute-start.4 = (f32[4,4,128]{2,1,0:T(4,128)S(1)}, f32[4,4,128]{2,1,0:T(4,128)S(1)}, u32[]{:S(2)}, u32[]{:S(2)}) collective-permute-start(f32[4,4,128]{2,1,0:T(4,128)S(1)} %pad_maximum_fusion.38), channel_id=1, source_target_pairs={{0,32},{32,64},{64,96},{96,128},{128,160},{160,192},{192,224},{224... | collective-permute-start | bytes 24584 | tf_op jit(solution)/shard_map/ppermute | solution.py:20
  246.1 14.3 %collective-permute-start.6 = (f32[4,12,4]{2,1,0:T(8,128)S(1)}, f32[4,12,4]{2,1,0:T(8,128)S(1)}, u32[]{:S(2)}, u32[]{:S(2)}) collective-permute-start(f32[4,12,4]{2,1,0:T(8,128)S(1)} %get-tuple-element.48), channel_id=1, source_target_pairs={{0,1},{1,2},{2,3},{3,4},{4,5},{5,6},{6,7},{7,8},{8,9},{9,10},{10,1... | collective-permute-start | bytes 2312 | tf_op jit(solution)/shard_map/ppermute | solution.py:20
  249.0 11.4 %collective-permute-start.7 = (f32[4,12,4]{2,1,0:T(8,128)S(1)}, f32[4,12,4]{2,1,0:T(8,128)S(1)}, u32[]{:S(2)}, u32[]{:S(2)}) collective-permute-start(f32[4,12,4]{2,1,0:T(8,128)S(1)} %get-tuple-element.49), channel_id=1, source_target_pairs={{1,0},{2,1},{3,2},{4,3},{5,4},{6,5},{7,6},{8,7},{9,8},{10,9},{11,1... | collective-permute-start | bytes 2312 | tf_op jit(solution)/shard_map/ppermute | solution.py:23
  298.2 7.0 %copy-start.9 = (f32[4096,256]{1,0:T(8,128)S(1)}, f32[4096,256]{1,0:T(8,128)}, u32[]{:S(2)}) copy-start(f32[4096,256]{1,0:T(8,128)} %get-tuple-element.94) | copy-start | bytes 12582916
  298.2 7.0 %copy-start.11 = (f32[4096,256]{1,0:T(8,128)S(1)}, f32[4096,256]{1,0:T(8,128)}, u32[]{:S(2)}) copy-start(f32[4096,256]{1,0:T(8,128)} %get-tuple-element.95) | copy-start | bytes 12582916
  305.3 4.1 %copy-start.13 = (f32[4096,256]{1,0:T(8,128)S(1)}, f32[4096,256]{1,0:T(8,128)}, u32[]{:S(2)}) copy-start(f32[4096,256]{1,0:T(8,128)} %get-tuple-element.96) | copy-start | bytes 12582916
  305.3 4.1 %copy-start.15 = (f32[4096,256]{1,0:T(8,128)S(1)}, f32[4096,256]{1,0:T(8,128)}, u32[]{:S(2)}) copy-start(f32[4096,256]{1,0:T(8,128)} %get-tuple-element.97) | copy-start | bytes 12582916
  309.4 4.1 %copy-start.1 = (f32[4096,256]{1,0:T(8,128)S(1)}, f32[4096,256]{1,0:T(8,128)}, u32[]{:S(2)}) copy-start(f32[4096,256]{1,0:T(8,128)} %get-tuple-element.102) | copy-start | bytes 12582916
  309.4 4.1 %copy-start.3 = (f32[4096,256]{1,0:T(8,128)S(1)}, f32[4096,256]{1,0:T(8,128)}, u32[]{:S(2)}) copy-start(f32[4096,256]{1,0:T(8,128)} %get-tuple-element.103) | copy-start | bytes 12582916
  332.0 7.0 %copy-start.5 = (f32[4096,256]{1,0:T(8,128)S(1)}, f32[4096,256]{1,0:T(8,128)}, u32[]{:S(2)}) copy-start(f32[4096,256]{1,0:T(8,128)} %get-tuple-element.92) | copy-start | bytes 12582916
  332.0 7.0 %copy-start.7 = (f32[4096,256]{1,0:T(8,128)S(1)}, f32[4096,256]{1,0:T(8,128)}, u32[]{:S(2)}) copy-start(f32[4096,256]{1,0:T(8,128)} %get-tuple-element.93) | copy-start | bytes 12582916
  339.0 22.4 %copy-start.17 = (f32[10,32,128]{2,1,0:T(8,128)S(1)}, f32[10,32,128]{2,1,0:T(8,128)}, u32[]{:S(2)}) copy-start(f32[10,32,128]{2,1,0:T(8,128)} %param.13) | copy-start | bytes 491524
